TPU v7x, 128 devices: a whole 4x4x4 slice. The times are simulated.
128 devices in a mesh: row: 4 (over z_hi, core), col: 32 (over x, z_lo, y).
Axes of the slice: x: 4, y: 4, z: 4 (z_hi: 2, z_lo: 2; z = z_hi * 2 + z_lo), core: 2. Of those that a mesh axis runs over, the one named last changes fastest.
Arguments:
- right_side: float32 [131072, 128], P(('row', 'col')), may hold values from -150 to 150
- block_values: bfloat16 [64, 917504], P(None, ('row', 'col')), may hold values from -1 to 2, as said below
- block_cols: int32 [14336], P(('row', 'col')), may hold values from 0 to 511, as said below
- row_ptrs: int32 [8320], P(('row', 'col')), may hold values from 0 to 112, as said below
- precond: float32 [131072, 1024], P(('row', 'col')), may hold values from -1 to 2, as said below
Outputs:
- solution: float32 [131072, 128], P(('row', 'col'))
- residual: float32 [131072, 128], P(('row', 'col'))
Inputs may be any that keep to these rules, and one draw needn't show every extreme that they name: `row_ptrs`: in each tile t the 65 pointers from index t * (65) on never fall, start at 0 and end at 112. `block_cols`: each of the 2048 block rows of A holds 7 blocks. `block_values`: with the pattern, the blocks form a symmetric matrix A. `precond`: each 1024 x 1024 block is lower triangular with a positive diagonal.
All inputs are finite; a program needn't handle non-finite values.
Results may differ from a plain program's by a relative error of at most 0.0076.
Values may be sent and summed in bfloat16 or wider, within the bound.
A program may use at most 128 MiB of HBM per device.

v0:
```python
import jax
import jax.numpy as jnp
from jax import lax
from jax.sharding import PartitionSpec as P

ITERS = 2


def per_device(right_side, block_values, block_cols, row_ptrs, precond):
    block_size = block_values.shape[0]
    slot_count = block_cols.shape[0]
    tile_rows = row_ptrs.shape[0] - 1
    seg_rows = right_side.shape[0]
    rhs_count = right_side.shape[1]
    tile_cols = lax.axis_size("col") * (seg_rows // block_size)
    tile_blocks = block_values.reshape(block_size, slot_count, block_size)
    slot_index = jnp.arange(slot_count, dtype=jnp.int32)
    slot_rows = jnp.sum((slot_index[:, None] >= row_ptrs[None, 1:]).astype(jnp.int32), axis=1)
    solution = jnp.zeros_like(right_side)
    residual = right_side
    direction = right_side
    image_vec = right_side
    alpha_prev = jnp.ones((rhs_count,), jnp.float32)
    gamma_prev = jnp.ones((rhs_count,), jnp.float32)
    for iteration in range(ITERS):
        half_step = jnp.dot(
            precond, residual, precision=lax.Precision.HIGHEST, preferred_element_type=jnp.float32
        )
        smoothed = lax.dot_general(
            precond,
            half_step,
            (((0,), (0,)), ((), ())),
            precision=lax.Precision.HIGHEST,
            preferred_element_type=jnp.float32,
        )
        local_energy = jnp.sum(residual * smoothed, axis=0)
        gamma_now = lax.psum(local_energy, ("row", "col"))
        gathered = lax.all_gather(smoothed.astype(jnp.bfloat16), "col", axis=0, tiled=True)
        pieces = gathered.reshape(tile_cols, block_size, rhs_count)[block_cols]
        products = jnp.einsum(
            "ibj,bjk->bik", tile_blocks, pieces, preferred_element_type=jnp.float32
        )
        partial_value = jax.ops.segment_sum(
            products, slot_rows, num_segments=tile_rows, indices_are_sorted=True
        )
        applied = lax.psum_scatter(
            partial_value.reshape(tile_rows * block_size, rhs_count),
            "row",
            scatter_dimension=0,
            tiled=True,
        )
        delta_now = lax.psum(jnp.sum(smoothed * applied, axis=0), ("row", "col"))
        if iteration == 0:
            alpha_now = gamma_now / delta_now
            direction = smoothed
            image_vec = applied
        else:
            beta_now = gamma_now / gamma_prev
            alpha_now = gamma_now / (delta_now - beta_now * gamma_now / alpha_prev)
            direction = smoothed + beta_now * direction
            image_vec = applied + beta_now * image_vec
        solution = solution + alpha_now * direction
        residual = residual - alpha_now * image_vec
        gamma_prev = gamma_now
        alpha_prev = alpha_now
    return (solution, residual)


def solution(mesh):
    return jax.shard_map(
        per_device,
        mesh=mesh,
        in_specs=(
            P(("row", "col"), None),
            P(None, ("row", "col")),
            P(("row", "col")),
            P(("row", "col")),
            P(("row", "col"), None),
        ),
        out_specs=(P(("row", "col"), None), P(("row", "col"), None)),
        check_vma=False,
    )
```

profile of v0, /device:TPU:1, one launch (start us, length us, event | category | flops | bytes accessed | tf_op | source)
XLA Modules:
  0.0 653.4 jit_solution(4864520073481413777)
XLA Ops:
  7.2 0.0 all-gather.3.cloned.1.call-start
  7.2 0.0 copy-start
  7.2 5.4 fusion.5
  12.7 0.0 copy-done
  12.7 0.0 copy-start.7
  12.7 3.2 fusion.3
  15.9 0.0 copy-start.8
  15.9 0.0 all-gather.3.cloned.1.call-update
  15.9 0.0 reduce-scatter.3.cloned.1.call-start
  16.0 0.0 copy-done.7
  16.0 0.1 slice.3
  16.0 2.3 reshape.24
  18.3 0.0 copy-done.8
  18.3 0.0 copy-start.2
  18.4 0.1 convert_reduce_fusion
  18.5 148.9 %all-gather.3.cloned.1.call-done = bf16[32768,128]{0,1:T(8,128)(2,1)} async-done(((bf16[1024,128]{0,1:T(8,128)(2,1)}), bf16[32768,128]{0,1:T(8,128)(2,1)}) %all-gather.3.cloned.1.call-update) | async-done | bytes 8388624 | tf_op jit(solution)/shard_map/all_gather | solution.py:38
  167.4 11.9 %copy.26 = bf16[32768,128]{1,0:T(8,128)(2,1)} copy(bf16[32768,128]{0,1:T(8,128)(2,1)} %all-gather.3.cloned.1.call-done) | data formatting | bytes 16777216 | tf_op jit(solution)/shard_map/all_gather | solution.py:38
  179.3 5.4 gather_fusion
  184.7 0.0 copy-done.2
  184.7 3.9 convolution_bitcast_fusion.1
  188.6 0.2 broadcast.13.clone
  188.9 11.9 %scatter_fusion = f32[64,64,128]{2,1,0:T(8,128)S(1)} fusion(f32[64,64,128]{2,1,0:T(8,128)S(1)} %broadcast.13.clone, s32[112]{0:T(128)S(1)} %convert_reduce_fusion, f32[112,64,128]{2,1,0:T(8,128)} %convolution_bitcast_fusion.1), kind=kCustom, calls=%fused_computation.2 | custom fusion | flops 917504 | bytes 11010496 | tf_op jit(solution)/shard_map/scatter-add | solution.py:43
  200.8 1.9 copy.28
  202.6 0.0 copy-start.6
  202.7 0.0 reduce-scatter.3.cloned.1.call-update
  202.7 0.0 all-gather.5.cloned.1.call-start
  202.7 1.0 copy-done.6
  203.7 0.2 copy.25
  203.9 57.5 %reduce-scatter.3.cloned.1.call-done = f32[1024,128]{0,1:T(8,128)} async-done(((f32[4096,128]{0,1:T(8,128)}), f32[1024,128]{0,1:T(8,128)}) %reduce-scatter.3.cloned.1.call-update) | async-done | bytes 524304 | tf_op jit(solution)/shard_map/reduce_scatter | solution.py:46
  261.4 1.2 multiply_reduce_fusion.2
  262.6 64.9 %all-reduce.1 = (f32[128]{0:T(128)S(1)}, f32[128]{0:T(128)S(1)}) all-reduce(f32[128]{0:T(128)S(1)} %get-tuple-element.11, f32[128]{0:T(128)S(1)} %get-tuple-element.10), channel_id=1, replica_groups=mesh['row'=4,'col'=32] {'row','col'}, use_global_device_ids=true, to_apply=%region_1.0 | all-reduce | flops 256 | bytes 2048 | tf_op jit(solution)/shard_map/psum | solution.py:37
  327.5 0.0 copy-start.1
  327.5 6.9 %fusion.2 = f32[128,1024]{1,0:T(8,128)S(1)} fusion(f32[1024,1024]{1,0:T(8,128)} %param.9, f32[1024,128]{0,1:T(8,128)S(1)} %copy.25, f32[1024,128]{0,1:T(8,128)} %reduce-scatter.3.cloned.1.call-done, f32[128]{0:T(128)S(1)} %div.12), kind=kOutput, calls=%fused_computation.22 | convolution fusion | flops 1610874880 | bytes 5767680 | tf_op jit(solution)/shard_map/dot_general | solution.py:26
  334.5 0.0 copy-done.1
  334.5 3.3 fusion.4
  337.8 0.0 all-gather.5.cloned.1.call-update
  337.8 0.0 reduce-scatter.5.cloned.1.call-start
  337.8 145.3 %all-gather.5.cloned.1.call-done = bf16[32768,128]{0,1:T(8,128)(2,1)} async-done(((bf16[1024,128]{0,1:T(8,128)(2,1)}), bf16[32768,128]{0,1:T(8,128)(2,1)}) %all-gather.5.cloned.1.call-update) | async-done | bytes 8388624 | tf_op jit(solution)/shard_map/all_gather | solution.py:38
  483.2 11.9 %copy.30 = bf16[32768,128]{1,0:T(8,128)(2,1)} copy(bf16[32768,128]{0,1:T(8,128)(2,1)} %all-gather.5.cloned.1.call-done) | data formatting | bytes 16777216 | tf_op jit(solution)/shard_map/all_gather | solution.py:38
  495.1 0.0 copy-start.3
  495.1 5.6 gather_fusion.1
  500.7 0.0 copy-done.3
  500.7 3.9 convolution_bitcast_fusion
  504.7 0.2 broadcast.13
  504.9 11.9 %scatter_fusion.1 = f32[64,64,128]{2,1,0:T(8,128)S(1)} fusion(f32[64,64,128]{2,1,0:T(8,128)S(1)} %broadcast.13, s32[112]{0:T(128)S(1)} %convert_reduce_fusion, f32[112,64,128]{2,1,0:T(8,128)} %convolution_bitcast_fusion), kind=kCustom, calls=%fused_computation.3 | custom fusion | flops 917504 | bytes 11010496 | tf_op jit(solution)/shard_map/scatter-add | solution.py:43
  516.8 1.9 copy.32
  518.7 0.0 copy-start.4
  518.7 0.0 copy-start.5
  518.7 0.0 reduce-scatter.5.cloned.1.call-update
  518.7 58.8 %reduce-scatter.5.cloned.1.call-done = f32[1024,128]{0,1:T(8,128)} async-done(((f32[4096,128]{0,1:T(8,128)}), f32[1024,128]{0,1:T(8,128)}) %reduce-scatter.5.cloned.1.call-update) | async-done | bytes 524304 | tf_op jit(solution)/shard_map/reduce_scatter | solution.py:46
  577.5 0.0 copy-done.4
  577.5 0.0 copy-done.5
  577.5 1.3 multiply_reduce_fusion
  578.7 64.7 %all-reduce = (f32[128]{0:T(128)S(1)}, f32[128]{0:T(128)S(1)}) all-reduce(f32[128]{0:T(128)S(1)} %get-tuple-element.9, f32[128]{0:T(128)S(1)} %get-tuple-element.8), channel_id=1, replica_groups=mesh['row'=4,'col'=32] {'row','col'}, use_global_device_ids=true, to_apply=%region_8.0 | all-reduce | flops 256 | bytes 2048 | tf_op jit(solution)/shard_map/psum | solution.py:37
  643.5 1.4 multiply_subtract_fusion
  644.9 1.0 copy.34
  645.9 1.0 copy.33
  (4 shorter events, 0.0 us)
Async XLA Ops:
  7.2 160.2 %all-gather.3.cloned.1.call-start = ((), (), s32[]{:S(2)}) async-start(), calls=%async_computation.2 | async-start | bytes 8650752 | tf_op jit(solution)/shard_map/all_gather | solution.py:38
  7.2 5.5 copy-start
  12.7 3.3 copy-start.7
  15.9 2.4 copy-start.8
  15.9 245.5 %reduce-scatter.3.cloned.1.call-start = ((), (), s32[]{:S(2)}) async-start(), calls=%async_computation.3 | async-start | bytes 2621440 | tf_op jit(solution)/shard_map/reduce_scatter | solution.py:46
  18.3 166.4 %copy-start.2 = (bf16[64,112,64]{2,1,0:T(8,128)(2,1)}, bf16[64,112,64]{2,1,0:T(8,128)(2,1)S(1)}, u32[]{:S(2)}) copy-start(bf16[64,112,64]{2,1,0:T(8,128)(2,1)S(1)} %reshape.24) | copy-start | bytes 2752516
  202.6 1.0 copy-start.6
  202.7 280.5 %all-gather.5.cloned.1.call-start = ((), (), s32[]{:S(2)}) async-start(), calls=%async_computation.4 | async-start | bytes 8650752 | tf_op jit(solution)/shard_map/all_gather | solution.py:38
  327.5 6.9 %copy-start.1 = (f32[1024,1024]{1,0:T(8,128)S(1)}, f32[1024,1024]{1,0:T(8,128)}, u32[]{:S(2)}) copy-start(f32[1024,1024]{1,0:T(8,128)} %param.9) | copy-start | bytes 12582916
  337.8 239.7 %reduce-scatter.5.cloned.1.call-start = ((), (), s32[]{:S(2)}) async-start(), calls=%async_computation.5 | async-start | bytes 2621440 | tf_op jit(solution)/shard_map/reduce_scatter | solution.py:46
  495.1 5.6 copy-start.3
  518.7 58.8 %copy-start.4 = (f32[1024,128]{0,1:T(8,128)S(1)}, f32[1024,128]{0,1:T(8,128)}, u32[]{:S(2)}) copy-start(f32[1024,128]{0,1:T(8,128)} %reduce-scatter.3.cloned.1.call-done) | copy-start | bytes 1572868
  518.7 58.8 %copy-start.5 = (f32[1024,128]{0,1:T(8,128)S(1)}, f32[1024,128]{0,1:T(8,128)}, u32[]{:S(2)}) copy-start(f32[1024,128]{0,1:T(8,128)} %get-tuple-element.23) | copy-start | bytes 1572868
Sparse Core Ops, SparseCore 0:
  16.0 151.3 all-gather.2
  202.8 58.5 reduce-scatter.2
  337.9 145.2 all-gather.4
  518.8 58.5 reduce-scatter.4
where the time goes:
time: 655 us; the launch traced here: 653 us
  waiting for transfers between devices  411 us (63%)
  blocking collectives  130 us (20%)
  local copies, waits for them, and re-layouts  44.6 us (7%)
  other arithmetic  27.8 us (4%)
  matrix products  26.7 us (4%)
  between operations  13.9 us (2%)
    all_gather x2, waiting for transfers between devices, per_device(): lax.all_gather(smoothed.astype(jnp.bfloat16), 'col', axis=0, tiled=True)  294 us
    psum x2, blocking collectives, per_device(): gamma_now = lax.psum(local_energy, ('row', 'col'))  130 us
    reduce_scatter x2, waiting for transfers between devices, per_device(): lax.psum_scatter(partial_value.reshape(tile_rows * block_size, rhs_count)...  116 us
    scatter-add x2, other arithmetic, per_device(): jax.ops.segment_sum(products, slot_rows, num_segments=tile_rows, indices_...  23.8 us
    all_gather x2, local copies, waits for them, and re-layouts, per_device(): lax.all_gather(smoothed.astype(jnp.bfloat16), 'col', axis=0, tiled=True)  23.8 us
  transfers between devices with their start and end apart: 4, of which 4 were waited for; matrix products, arithmetic and copies ran while one was open for 0% of the time, Pallas kernels for 0%

commit v1 on v0

v1 whole, which is shorter than its diff:
```python
import heapq

import jax
import jax.numpy as jnp
from jax import lax
from jax.experimental import pallas as pl
from jax.experimental.pallas import tpu as pltpu
from jax.sharding import PartitionSpec as P

ITERS = 2
MESH = pl.DeviceIdType.MESH
RING = {"x": 4, "z": 2, "y": 4}
DIMS = ("x", "z", "y")
PARTS = ((("z", "y", "x"), 0, 512), (("z", "x", "y"), 512, 512))
LINK_RATE = 46e3 / 256
HOP = 1.7


def shifted(offset, dim, step):
    pos = DIMS.index(dim)
    changed = list(offset)
    changed[pos] = (changed[pos] + step) % RING[dim]
    return tuple(changed)


def sends_of(part, offset, stage):
    order, start, count = PARTS[part]
    half = count // 2
    out = []
    if stage >= 0 and order[stage] != "z":
        dim = order[stage]
        value = offset[DIMS.index(dim)]
        if value == 3:
            out.append((dim, 1, start, half, (part, shifted(offset, dim, -1), "p")))
        if value == 1:
            out.append((dim, -1, start + half, half, (part, shifted(offset, dim, 1), "m")))
    for later in range(stage + 1, 3):
        dim = order[later]
        out.append((dim, 1, start, count, (part, shifted(offset, dim, -1), "f")))
        if dim != "z":
            out.append((dim, -1, start, count, (part, shifted(offset, dim, 1), "f")))
    return out


def last_stage(part, offset):
    order = PARTS[part][0]
    return max(j for j in range(3) if offset[DIMS.index(order[j])] != 0)


def gather_plan():
    heap, free, ids, plan = [], {}, {}, []

    def issue(now, offset, sends):
        for dim, step, start, count, key in sends:
            link = (dim, step)
            free[link] = max(free.get(link, 0.0), now) + count / LINK_RATE
            ids[key] = len(ids)
            heapq.heappush(heap, (free[link] + HOP, ids[key], key, start, count))

    first = []
    for part in range(len(PARTS)):
        first += [(j, s) for j, s in enumerate(sends_of(part, (0, 0, 0), -1))]
    first = [s for _, s in sorted(first, key=lambda item: item[0])]
    issue(0.0, (0, 0, 0), first)
    plan.append((None, (0, 0, 0), 0, 0, first))
    halves = set()
    while heap:
        now, _, key, start, count = heapq.heappop(heap)
        part, offset, kind = key
        stage = last_stage(part, offset)
        sends = []
        if kind == "f":
            sends = sends_of(part, offset, stage)
        elif (part, offset) in halves:
            sends = sends_of(part, offset, stage)
        else:
            halves.add((part, offset))
        issue(now, offset, sends)
        plan.append((key, offset, start, count, sends))
    return plan, ids


PLAN, COPY_IDS = gather_plan()
COPIES = len(COPY_IDS)


def position():
    row = lax.axis_index("row")
    col = lax.axis_index("col")
    return {
        "h": row // 2, "core": row % 2,
        "x": col // 8, "z": (col // 4) % 2, "y": col % 4,
    }


def device_at(pos):
    return (pos["h"] * 2 + pos["core"], (pos["x"] * 2 + pos["z"]) * 4 + pos["y"])


def col_at(pos, offset):
    x, z, y = ((pos[d] + o) % RING[d] for d, o in zip(DIMS, offset))
    return (x * 2 + z) * 4 + y


def neighbour(pos, dim, step):
    moved = dict(pos)
    moved[dim] = (pos[dim] + step) % RING[dim]
    return device_at(moved)


def gather_kernel(own_ref, all_ref, send_sems, recv_sems, local_sem):
    pos = position()
    barrier = pltpu.get_barrier_semaphore()
    peers = [neighbour(pos, d, s) for d, s in (("x", 1), ("x", -1), ("y", 1), ("y", -1), ("z", 1))]
    for peer in peers:
        pl.semaphore_signal(barrier, inc=1, device_id=peer, device_id_type=MESH)
    pl.semaphore_wait(barrier, len(peers))
    mine = pltpu.make_async_copy(own_ref, all_ref.at[col_at(pos, (0, 0, 0))], local_sem)
    mine.start()
    started = []
    for key, offset, start, count, sends in PLAN:
        slot = all_ref.at[col_at(pos, offset)]
        if key is not None:
            view = slot.at[pl.ds(start, count)]
            pltpu.make_async_remote_copy(
                src_ref=view, dst_ref=view,
                send_sem=send_sems.at[COPY_IDS[key]], recv_sem=recv_sems.at[COPY_IDS[key]],
                device_id=peers[0], device_id_type=MESH,
            ).wait_recv()
        for dim, step, s0, n, target in sends:
            source = (own_ref if key is None else slot).at[pl.ds(s0, n)]
            copy = pltpu.make_async_remote_copy(
                src_ref=source, dst_ref=slot.at[pl.ds(s0, n)],
                send_sem=send_sems.at[COPY_IDS[target]], recv_sem=recv_sems.at[COPY_IDS[target]],
                device_id=neighbour(pos, dim, step), device_id_type=MESH,
            )
            copy.start()
            started.append(copy)
    for copy in started:
        copy.wait_send()
    mine.wait()


def gather_all(own):
    rows, rhs = own.shape
    return pl.pallas_call(
        gather_kernel,
        out_shape=jax.ShapeDtypeStruct((32, rows, rhs), own.dtype),
        in_specs=[pl.BlockSpec(memory_space=pl.ANY)],
        out_specs=pl.BlockSpec(memory_space=pl.ANY),
        scratch_shapes=[
            pltpu.SemaphoreType.DMA((COPIES,)), pltpu.SemaphoreType.DMA((COPIES,)), pltpu.SemaphoreType.DMA,
        ],
        compiler_params=pltpu.CompilerParams(collective_id=0, has_side_effects=True),
        name="gather_all",
    )(own)


def product_kernel(cols_ref, fresh_ref, ptrs_ref, values_ref, all_ref, out_ref, pieces, running, sems):
    slots = pieces.shape[0]
    size = pieces.shape[1]

    def fetch(e):
        return pltpu.make_async_copy(all_ref.at[cols_ref[e]], pieces.at[e], sems.at[e])

    @pl.loop(0, slots)
    def _(e):
        fetch(e).start()

    def pair(t, acc):
        e = t * 2
        fetch(e).wait()
        fetch(e + 1).wait()
        both = values_ref[:, pl.ds(pl.multiple_of(e * size, 2 * size), 2 * size)]
        zero = jnp.zeros((size, pieces.shape[2]), pieces.dtype)
        right = jnp.concatenate(
            [jnp.concatenate([pieces[e], zero], axis=1), jnp.concatenate([zero, pieces[e + 1]], axis=1)], axis=0
        )
        product = jnp.dot(both, right, preferred_element_type=jnp.float32)
        width = pieces.shape[2]
        for k in range(2):
            acc = jnp.where(fresh_ref[e + k] == 1, 0.0, acc) + product[:, k * width:(k + 1) * width]
            running[e + k] = acc
        return acc

    lax.fori_loop(0, slots // 2, pair, jnp.zeros(running.shape[1:], jnp.float32), unroll=4)

    @pl.loop(0, out_ref.shape[0])
    def _(l):
        end = ptrs_ref[l + 1]
        keep = end > ptrs_ref[l]
        value = running[jnp.maximum(end - 1, 0)]
        out_ref[l] = jnp.where(keep, value, 0.0)


def block_products(cols, fresh, ptrs, values, gathered):
    size = values.shape[0]
    slots = cols.shape[0]
    rhs = gathered.shape[-1]
    pieces = gathered.reshape(-1, size, rhs)
    tile_rows = ptrs.shape[0] - 1
    return pl.pallas_call(
        product_kernel,
        out_shape=jax.ShapeDtypeStruct((tile_rows, size, rhs), jnp.float32),
        in_specs=[pl.BlockSpec(memory_space=pltpu.SMEM)] * 3
        + [pl.BlockSpec(memory_space=pltpu.VMEM), pl.BlockSpec(memory_space=pl.ANY)],
        out_specs=pl.BlockSpec(memory_space=pltpu.VMEM),
        scratch_shapes=[
            pltpu.VMEM((slots, size, rhs), jnp.bfloat16),
            pltpu.VMEM((slots, size, rhs), jnp.float32),
            pltpu.SemaphoreType.DMA((slots,)),
        ],
        name="block_products",
    )(cols, fresh, ptrs, values, pieces)


CHUNKS = 4


def reduce_kernel(part_ref, smoothed_ref, residual_ref, applied_ref, stats_ref,
                  from_core, far, relay, landed, mine, others,
                  core_send, core_recv, relay_send, relay_recv, far_send, far_recv, sum_send, sum_recv):
    pos = position()
    h, core, z = pos["h"], pos["core"], pos["z"]
    height = h * 2 + z

    def along_z(step):
        moved = dict(pos)
        level = (height + step) % 4
        moved["h"], moved["z"] = level // 2, level % 2
        return device_at(moved)

    partner = device_at({**pos, "core": 1 - core})
    groups = [
        [partner],
        [along_z(s) for s in (1, 2, 3)],
        [neighbour(pos, "x", s) for s in (1, 2, 3)],
        [neighbour(pos, "y", s) for s in (1, 2, 3)],
    ]
    barrier = pltpu.get_barrier_semaphore()
    peers = [p for g in groups for p in g]
    for peer in peers:
        pl.semaphore_signal(barrier, inc=1, device_id=peer, device_id_type=MESH)
    pl.semaphore_wait(barrier, len(peers))

    swaps = []
    for k, level in enumerate((1 - h, h)):
        copy = pltpu.make_async_remote_copy(
            src_ref=part_ref.at[level * 2 + 1 - core], dst_ref=from_core.at[k],
            send_sem=core_send.at[k], recv_sem=core_recv.at[k], device_id=partner, device_id_type=MESH,
        )
        copy.start()
        swaps.append(copy)
    rows = part_ref.shape[1]
    step_rows = rows // CHUNKS
    swaps[0].wait_recv()
    order = [c for pair in zip(range(CHUNKS // 2), range(CHUNKS // 2, CHUNKS)) for c in pair]
    hops = {}
    for c in order:
        span = pl.ds(c * step_rows, step_rows)
        far[c] = part_ref[(1 - h) * 2 + core, span, :] + from_core[0, span, :]
    for c in order:
        direction = 1 if c < CHUNKS // 2 else 3
        hops[c] = pltpu.make_async_remote_copy(
            src_ref=far.at[c], dst_ref=relay.at[c],
            send_sem=relay_send.at[c], recv_sem=relay_recv.at[c],
            device_id=along_z(direction), device_id_type=MESH,
        )
        hops[c].start()
    ends = {}
    for c in order:
        direction = 1 if c < CHUNKS // 2 else 3
        hops[c].wait_recv()
        ends[c] = pltpu.make_async_remote_copy(
            src_ref=relay.at[c], dst_ref=landed.at[c],
            send_sem=far_send.at[c], recv_sem=far_recv.at[c],
            device_id=along_z(direction), device_id_type=MESH,
        )
        ends[c].start()
    gamma = jnp.sum(residual_ref[...] * smoothed_ref[...], axis=0, keepdims=True)
    swaps[1].wait_recv()
    delta = jnp.zeros_like(gamma)
    for c in order:
        span = pl.ds(c * step_rows, step_rows)
        ends[c].wait_recv()
        value = part_ref[h * 2 + core, span, :] + from_core[1, span, :] + landed[c]
        applied_ref[span, :] = value
        delta = delta + jnp.sum(smoothed_ref[span, :] * value, axis=0, keepdims=True)
    total = jnp.concatenate([gamma, delta, jnp.zeros((6, gamma.shape[1]), jnp.float32)], axis=0)
    sums = []
    base = 0
    for g, group in enumerate(groups):
        mine[g] = total
        batch = []
        for k, peer in enumerate(group):
            copy = pltpu.make_async_remote_copy(
                src_ref=mine.at[g], dst_ref=others.at[base + k],
                send_sem=sum_send.at[base + k], recv_sem=sum_recv.at[base + k],
                device_id=peer, device_id_type=MESH,
            )
            copy.start()
            batch.append(copy)
        for k, copy in enumerate(batch):
            copy.wait_recv()
            total = total + others[base + k]
        sums += batch
        base += len(group)
    stats_ref[...] = total
    for copy in swaps + list(hops.values()) + list(ends.values()) + sums:
        copy.wait_send()


def reduce_all(partial, smoothed, residual):
    rows, rhs = smoothed.shape
    dma = pltpu.SemaphoreType.DMA
    chunk = (CHUNKS, rows // CHUNKS, rhs)
    return pl.pallas_call(
        reduce_kernel,
        out_shape=(
            jax.ShapeDtypeStruct((rows, rhs), jnp.float32),
            jax.ShapeDtypeStruct((8, rhs), jnp.float32),
        ),
        in_specs=[pl.BlockSpec(memory_space=pltpu.VMEM)] * 3,
        out_specs=(pl.BlockSpec(memory_space=pltpu.VMEM),) * 2,
        scratch_shapes=[
            pltpu.VMEM((2, rows, rhs), jnp.float32),
            pltpu.VMEM(chunk, jnp.float32),
            pltpu.VMEM(chunk, jnp.float32),
            pltpu.VMEM(chunk, jnp.float32),
            pltpu.VMEM((4, 8, rhs), jnp.float32),
            pltpu.VMEM((10, 8, rhs), jnp.float32),
            dma((2,)), dma((2,)), dma((CHUNKS,)), dma((CHUNKS,)), dma((CHUNKS,)), dma((CHUNKS,)),
            dma((10,)), dma((10,)),
        ],
        compiler_params=pltpu.CompilerParams(collective_id=1, has_side_effects=True),
        name="reduce_all",
    )(partial, smoothed, residual)


def per_device(right_side, block_values, block_cols, row_ptrs, precond):
    slot_count = block_cols.shape[0]
    seg_rows, rhs_count = right_side.shape
    slot_index = jnp.arange(slot_count, dtype=jnp.int32)
    fresh = jnp.any(slot_index[:, None] == row_ptrs[None, :-1], axis=1).astype(jnp.int32)
    solution = jnp.zeros_like(right_side)
    residual = right_side
    for iteration in range(ITERS):
        half_step = jnp.dot(
            precond, residual, precision=lax.Precision.HIGHEST, preferred_element_type=jnp.float32
        )
        smoothed = lax.dot_general(
            precond, half_step, (((0,), (0,)), ((), ())),
            precision=lax.Precision.HIGHEST, preferred_element_type=jnp.float32,
        )
        gathered = gather_all(smoothed.astype(jnp.bfloat16))
        partial = block_products(block_cols, fresh, row_ptrs, block_values, gathered)
        applied, stats = reduce_all(partial.reshape(4, seg_rows, rhs_count), smoothed, residual)
        gamma_now, delta_now = stats[0], stats[1]
        if iteration == 0:
            alpha_now = gamma_now / delta_now
            direction = smoothed
            image_vec = applied
        else:
            beta_now = gamma_now / gamma_prev
            alpha_now = gamma_now / (delta_now - beta_now * gamma_now / alpha_prev)
            direction = smoothed + beta_now * direction
            image_vec = applied + beta_now * image_vec
        solution = solution + alpha_now * direction
        residual = residual - alpha_now * image_vec
        gamma_prev = gamma_now
        alpha_prev = alpha_now
    return (solution, residual)


def solution(mesh):
    return jax.shard_map(
        per_device,
        mesh=mesh,
        in_specs=(
            P(("row", "col"), None),
            P(None, ("row", "col")),
            P(("row", "col")),
            P(("row", "col")),
            P(("row", "col"), None),
        ),
        out_specs=(P(("row", "col"), None), P(("row", "col"), None)),
        check_vma=False,
    )
```

time: 655 us -> 228 us (0.35)
  waiting for transfers between devices: 411 us -> 0 us
  Pallas kernels: 0 us -> 191 us
  blocking collectives: 130 us -> 0 us
  local copies, waits for them, and re-layouts: 44.6 us -> 0.05 us
  other arithmetic: 27.8 us -> 6.56 us
  between operations: 13.9 us -> 0.81 us
    all_gather x2 -> x0, waiting for transfers between devices: 294 us -> none  [per_device(): lax.all_gather(smoothed.astype(jnp.bfloat16), 'col', axis=0, tiled=True)]
    pallas_call x0 -> x6, Pallas kernels: none -> 191 us  [the longest x2 101 us: gather_all(): pl.pallas_call(gather_kernel, out_shape=jax.ShapeDtypeStruct((32, rows, r...]
    psum x2 -> x0, blocking collectives: 130 us -> none  [per_device(): gamma_now = lax.psum(local_energy, ('row', 'col'))]
    reduce_scatter x2 -> x0, waiting for transfers between devices: 116 us -> none  [per_device(): lax.psum_scatter(partial_value.reshape(tile_rows * block_size, rhs_count)...]
    scatter-add x2 -> x0, other arithmetic: 23.8 us -> none  [per_device(): jax.ops.segment_sum(products, slot_rows, num_segments=tile_rows, indices_...]
    all_gather x2 -> x0, local copies, waits for them, and re-layouts: 23.8 us -> none  [per_device(): lax.all_gather(smoothed.astype(jnp.bfloat16), 'col', axis=0, tiled=True)]
    gather x2 -> x0, local copies, waits for them, and re-layouts: 11.1 us -> none  [per_device(): pieces = gathered.reshape(tile_cols, block_size, rhs_count)[block_cols]]
    dot_general x2, matrix products: 6.47 us -> 15.4 us  [per_device(): lax.dot_general(precond, half_step, (((0,), (0,)), ((), ())), precision=l...]
  transfers between devices with their start and end apart: 4 -> 0, of which waited for: 4 -> 0; matrix products, arithmetic and copies ran while one was open for 0% -> 0% of each run, Pallas kernels for 0% -> 0%
where the time goes in v1:
time: 228 us; the launch traced here: 226 us
  Pallas kernels  191 us (84%)
  matrix products  27.5 us (12%)
  other arithmetic  6.56 us (3%)
    pallas_call x2, Pallas kernels, gather_all(): pl.pallas_call(gather_kernel, out_shape=jax.ShapeDtypeStruct((32, rows, r...  101 us
    pallas_call x2, Pallas kernels, reduce_all(): pl.pallas_call(reduce_kernel, out_shape=(jax.ShapeDtypeStruct((rows, rhs)...  63.4 us
    pallas_call x2, Pallas kernels, block_products(): pl.pallas_call(product_kernel, out_shape=jax.ShapeDtypeStruct((tile_rows,...  27.2 us
    dot_general x2, matrix products, per_device(): lax.dot_general(precond, half_step, (((0,), (0,)), ((), ())), precision=l...  15.4 us
    dot_general x2, matrix products, per_device(): jnp.dot(precond, residual, precision=lax.Precision.HIGHEST, preferred_ele...  12.2 us

profile of v1, /device:TPU:1, one launch (start us, length us, event | category | flops | bytes accessed | tf_op | source)
XLA Modules:
  0.0 226.0 jit_solution(15258395420919789462)
XLA Ops:
  0.6 0.0 copy-start
  0.6 0.9 fusion
  1.5 0.6 convert_element_type.9.fresh_ref
  2.1 5.3 %fusion.4 = f32[1024,128]{1,0:T(8,128)S(1)} fusion(f32[1024,1024]{1,0:T(8,128)} %param.9, f32[1024,128]{1,0:T(8,128)} %residual_ref.1), kind=kOutput, calls=%fused_computation.13 | convolution fusion | flops 1610612736 | bytes 5242880 | tf_op jit(solution)/shard_map/dot_general | solution.py:348
  7.5 0.0 copy-done
  7.5 7.7 %fusion.2 = (bf16[1024,128]{1,0:T(8,128)(2,1)}, f32[1024,128]{1,0:T(8,128)}) fusion(f32[1024,128]{1,0:T(8,128)S(1)} %fusion.4, f32[1024,1024]{1,0:T(8,128)S(1)} %copy-done), kind=kOutput, calls=%fused_computation.11 | convolution fusion | flops 1610743808 | bytes 5505024 | tf_op jit(solution)/shard_map/dot_general | solution.py:351
  15.1 52.4 %gather_all.2 = bf16[32,1024,128]{2,1,0:T(8,128)(2,1)} custom-call(bf16[1024,128]{1,0:T(8,128)(2,1)} %get-tuple-element.14.own_ref), custom_call_target="tpu_custom_call" | custom-call | tf_op jit(solution)/shard_map/gather_all/pallas_call | solution.py:146
  67.6 0.0 copy-start.4
  67.6 13.6 %block_products.2 = f32[64,64,128]{2,1,0:T(8,128)} custom-call(s32[112]{0:T(128)} %cols_ref.3, s32[112]{0:T(128)} %convert_element_type.9.fresh_ref, s32[65]{0:T(128)} %ptrs_ref.3, bf16[64,7168]{1,0:T(8,128)(2,1)} %values_ref.3, bf16[512,64,128]{2,1,0:T(8,128)(2,1)} %bitcast.23), custom_call_target="tpu_custom_call" | custom-call | tf_op jit(solution)/shard_map/block_products/pallas_call | solution.py:202
  81.2 31.2 %reduce_all.2 = (f32[1024,128]{1,0:T(8,128)}, f32[8,128]{1,0:T(8,128)}) custom-call(f32[4,1024,128]{2,1,0:T(8,128)} %bitcast.25, f32[1024,128]{1,0:T(8,128)} %get-tuple-element.15.smoothed_ref, f32[1024,128]{1,0:T(8,128)} %residual_ref.1), custom_call_target="tpu_custom_call" | custom-call | tf_op jit(solution)/shard_map/reduce_all/pallas_call | solution.py:317
  112.4 0.0 copy-start.1
  112.4 0.8 divide_bitcast_fusion
  113.3 0.0 copy-done.4
  113.3 1.3 multiply_subtract_fusion.1.residual_ref
  114.6 0.0 copy-start.2
  114.6 6.9 %fusion.5 = f32[128,1024]{1,0:T(8,128)S(1)} fusion(f32[1024,128]{1,0:T(8,128)S(1)} %multiply_subtract_fusion.1.residual_ref, f32[1024,1024]{1,0:T(8,128)} %param.9), kind=kOutput, calls=%fused_computation.14 | convolution fusion | flops 1610612736 | bytes 5242880 | tf_op jit(solution)/shard_map/dot_general | solution.py:348
  121.4 0.0 copy-done.1
  121.5 7.7 %fusion.3 = (bf16[1024,128]{1,0:T(8,128)(2,1)}, f32[1024,128]{1,0:T(8,128)}) fusion(f32[128,1024]{1,0:T(8,128)S(1)} %fusion.5, f32[1024,1024]{1,0:T(8,128)S(1)} %copy-done.1), kind=kOutput, calls=%fused_computation.12 | convolution fusion | flops 1610743808 | bytes 5505024 | tf_op jit(solution)/shard_map/dot_general | solution.py:351
  129.2 0.0 copy-done.2
  129.2 48.1 %gather_all.3 = bf16[32,1024,128]{2,1,0:T(8,128)(2,1)} custom-call(bf16[1024,128]{1,0:T(8,128)(2,1)} %get-tuple-element.16.own_ref), custom_call_target="tpu_custom_call" | custom-call | tf_op jit(solution)/shard_map/gather_all/pallas_call | solution.py:146
  177.2 0.0 copy-start.3
  177.3 0.0 copy-start.5
  177.3 0.0 copy-start.6
  177.3 0.0 copy-start.7
  177.3 13.6 %block_products.3 = f32[64,64,128]{2,1,0:T(8,128)} custom-call(s32[112]{0:T(128)} %cols_ref.3, s32[112]{0:T(128)} %convert_element_type.9.fresh_ref, s32[65]{0:T(128)} %ptrs_ref.3, bf16[64,7168]{1,0:T(8,128)(2,1)} %values_ref.3, bf16[512,64,128]{2,1,0:T(8,128)(2,1)} %bitcast.22), custom_call_target="tpu_custom_call" | custom-call | tf_op jit(solution)/shard_map/block_products/pallas_call | solution.py:202
  190.8 32.2 %reduce_all.3 = (f32[1024,128]{1,0:T(8,128)}, f32[8,128]{1,0:T(8,128)}) custom-call(f32[4,1024,128]{2,1,0:T(8,128)} %bitcast.24, f32[1024,128]{1,0:T(8,128)} %get-tuple-element.17.smoothed_ref, f32[1024,128]{1,0:T(8,128)} %copy-done.2), custom_call_target="tpu_custom_call" | custom-call | tf_op jit(solution)/shard_map/reduce_all/pallas_call | solution.py:317
  223.1 0.8 fusion.1
  223.8 0.0 copy-done.3
  223.8 0.0 copy-done.5
  223.8 0.0 copy-done.6
  223.9 0.0 copy-done.7
  223.9 2.2 multiply_subtract_fusion
Async XLA Ops:
  0.6 6.8 %copy-start = (f32[1024,1024]{1,0:T(8,128)S(1)}, f32[1024,1024]{1,0:T(8,128)}, u32[]{:S(2)}) copy-start(f32[1024,1024]{1,0:T(8,128)} %param.9) | copy-start | bytes 12582916
  67.6 45.7 %copy-start.4 = (f32[1024,128]{1,0:T(8,128)S(1)}, f32[1024,128]{1,0:T(8,128)}, u32[]{:S(2)}) copy-start(f32[1024,128]{1,0:T(8,128)} %residual_ref.1) | copy-start | bytes 1572868
  112.4 9.0 %copy-start.1 = (f32[1024,1024]{1,0:T(8,128)S(1)}, f32[1024,1024]{1,0:T(8,128)}, u32[]{:S(2)}) copy-start(f32[1024,1024]{1,0:T(8,128)} %param.9) | copy-start | bytes 12582916
  114.6 14.6 %copy-start.2 = (f32[1024,128]{1,0:T(8,128)}, f32[1024,128]{1,0:T(8,128)S(1)}, u32[]{:S(2)}) copy-start(f32[1024,128]{1,0:T(8,128)S(1)} %multiply_subtract_fusion.1.residual_ref) | copy-start | bytes 1572868
  177.2 46.6 %copy-start.3 = (f32[1024,128]{1,0:T(8,128)S(1)}, f32[1024,128]{1,0:T(8,128)}, u32[]{:S(2)}) copy-start(f32[1024,128]{1,0:T(8,128)} %copy-done.2) | copy-start | bytes 1572868
  177.3 46.6 %copy-start.5 = (f32[1024,128]{1,0:T(8,128)S(1)}, f32[1024,128]{1,0:T(8,128)}, u32[]{:S(2)}) copy-start(f32[1024,128]{1,0:T(8,128)} %get-tuple-element.15.smoothed_ref) | copy-start | bytes 1572868
  177.3 46.6 %copy-start.6 = (f32[1024,128]{1,0:T(8,128)S(1)}, f32[1024,128]{1,0:T(8,128)}, u32[]{:S(2)}) copy-start(f32[1024,128]{1,0:T(8,128)} %get-tuple-element.17.smoothed_ref) | copy-start | bytes 1572868
  177.3 46.6 %copy-start.7 = (f32[1024,128]{1,0:T(8,128)S(1)}, f32[1024,128]{1,0:T(8,128)}, u32[]{:S(2)}) copy-start(f32[1024,128]{1,0:T(8,128)} %get-tuple-element.7) | copy-start | bytes 1572868

commit v2 on v1

v2 whole, which is shorter than its diff:
```python
import functools
import heapq

import jax
import jax.numpy as jnp
from jax import lax
from jax.experimental import pallas as pl
from jax.experimental.pallas import tpu as pltpu
from jax.sharding import PartitionSpec as P

MESH = pl.DeviceIdType.MESH
RING = {"x": 4, "z": 2, "y": 4}
DIMS = ("x", "z", "y")
PARTS = (
    (("z", "y", "x"), 0, 352),
    (("z", "x", "y"), 352, 352),
    (("y", "x", "z"), 704, 160),
    (("x", "y", "z"), 864, 160),
)
LINK_RATE = 46e3 / 256
HOP = 1.7
STRIPS = 4
GROUP = 16


def shifted(offset, dim, step):
    pos = DIMS.index(dim)
    changed = list(offset)
    changed[pos] = (changed[pos] + step) % RING[dim]
    return tuple(changed)


def sends_of(part, offset, stage):
    order, start, count = PARTS[part]
    half = count // 2
    out = []
    if stage >= 0 and order[stage] != "z":
        dim = order[stage]
        value = offset[DIMS.index(dim)]
        if value == 3:
            out.append((dim, 1, start, half, (part, shifted(offset, dim, -1), "p")))
        if value == 1:
            out.append((dim, -1, start + half, half, (part, shifted(offset, dim, 1), "m")))
    for later in range(stage + 1, 3):
        dim = order[later]
        out.append((dim, 1, start, count, (part, shifted(offset, dim, -1), "f")))
        if dim != "z":
            out.append((dim, -1, start, count, (part, shifted(offset, dim, 1), "f")))
    return out


def last_stage(part, offset):
    order = PARTS[part][0]
    return max(j for j in range(3) if offset[DIMS.index(order[j])] != 0)


def gather_plan():
    heap, free, ids, plan = [], {}, {}, []

    def issue(now, offset, sends):
        for dim, step, start, count, key in sends:
            link = (dim, step)
            free[link] = max(free.get(link, 0.0), now) + count / LINK_RATE
            ids[key] = len(ids)
            heapq.heappush(heap, (free[link] + HOP, ids[key], key, start, count))

    first = []
    for part in range(len(PARTS)):
        first += [(j, s) for j, s in enumerate(sends_of(part, (0, 0, 0), -1))]
    first = [s for _, s in sorted(first, key=lambda item: item[0])]
    issue(0.0, (0, 0, 0), first)
    plan.append((None, (0, 0, 0), 0, 0, first))
    halves = set()
    while heap:
        now, _, key, start, count = heapq.heappop(heap)
        part, offset, kind = key
        stage = last_stage(part, offset)
        sends = []
        if kind == "f":
            sends = sends_of(part, offset, stage)
        elif (part, offset) in halves:
            sends = sends_of(part, offset, stage)
        else:
            halves.add((part, offset))
        issue(now, offset, sends)
        plan.append((key, offset, start, count, sends))
    return plan, ids


PLAN, COPY_IDS = gather_plan()
COPIES = len(COPY_IDS)


def position():
    row = lax.axis_index("row")
    col = lax.axis_index("col")
    return {
        "h": row // 2, "core": row % 2,
        "x": col // 8, "z": (col // 4) % 2, "y": col % 4,
    }


def device_at(pos):
    return (pos["h"] * 2 + pos["core"], (pos["x"] * 2 + pos["z"]) * 4 + pos["y"])


def col_at(pos, offset):
    x, z, y = ((pos[d] + o) % RING[d] for d, o in zip(DIMS, offset))
    return (x * 2 + z) * 4 + y


def split(value):
    high = value.astype(jnp.bfloat16)
    return high, (value - high.astype(jnp.float32)).astype(jnp.bfloat16)


def wide_dot(a, b):
    def dot(p, q):
        return jnp.dot(p, q, preferred_element_type=jnp.float32)
    return dot(a[0], b[0]) + (dot(a[0], b[1]) + dot(a[1], b[0]))


def factor_copies(factor_ref, factor, sems):
    rows = factor.shape[0]
    tall = rows // STRIPS
    return [
        pltpu.make_async_copy(
            factor_ref.at[pl.ds(i * tall, tall), pl.ds(0, (i + 1) * tall)],
            factor.at[pl.ds(i * tall, tall), pl.ds(0, (i + 1) * tall)],
            sems.at[i],
        )
        for i in range(STRIPS)
    ]


def precondition_strip(i, factor, vector, flipped):
    tall = factor.shape[0] // STRIPS
    wide = (i + 1) * tall
    strip = split(factor[pl.ds(i * tall, tall), pl.ds(0, wide)])
    inner = wide_dot(strip, (vector[0, pl.ds(0, wide), :], vector[1, pl.ds(0, wide), :]))
    outer = wide_dot(split(inner.T), strip)
    if i == STRIPS - 1:
        flipped[:, pl.ds(0, wide)] = outer
    else:
        flipped[:, pl.ds(0, wide)] = flipped[:, pl.ds(0, wide)] + outer


def precondition_kernel(factor_ref, vector_ref, out_ref, half_ref, factor, vector, flipped, sems):
    copies = factor_copies(factor_ref, factor, sems)
    for copy in reversed(copies):
        copy.start()
    vector[0], vector[1] = split(vector_ref[...])
    for i in reversed(range(STRIPS)):
        copies[i].wait()
        precondition_strip(i, factor, vector, flipped)
    result = flipped[...].T
    out_ref[...] = result
    half_ref[...] = result.astype(jnp.bfloat16)


def precondition(factor, vector):
    rows, rhs = vector.shape
    return pl.pallas_call(
        precondition_kernel,
        out_shape=(
            jax.ShapeDtypeStruct((rows, rhs), jnp.float32),
            jax.ShapeDtypeStruct((rows, rhs), jnp.bfloat16),
        ),
        in_specs=[pl.BlockSpec(memory_space=pl.ANY), pl.BlockSpec(memory_space=pltpu.VMEM)],
        out_specs=(pl.BlockSpec(memory_space=pltpu.VMEM),) * 2,
        scratch_shapes=[
            pltpu.VMEM((rows, rows), jnp.float32),
            pltpu.VMEM((2, rows, rhs), jnp.bfloat16),
            pltpu.VMEM((rhs, rows), jnp.float32),
            pltpu.SemaphoreType.DMA((STRIPS,)),
        ],
        name="precondition",
    )(factor, vector)


def neighbour(pos, dim, step):
    moved = dict(pos)
    moved[dim] = (pos[dim] + step) % RING[dim]
    return device_at(moved)


def gather_kernel(own_ref, all_ref, send_sems, recv_sems, local_sem):
    pos = position()
    barrier = pltpu.get_barrier_semaphore()
    peers = [neighbour(pos, d, s) for d, s in (("x", 1), ("x", -1), ("y", 1), ("y", -1), ("z", 1))]
    for peer in peers:
        pl.semaphore_signal(barrier, inc=1, device_id=peer, device_id_type=MESH)
    pl.semaphore_wait(barrier, len(peers))
    mine = pltpu.make_async_copy(own_ref, all_ref.at[col_at(pos, (0, 0, 0))], local_sem)
    mine.start()
    started = []
    for key, offset, start, count, sends in PLAN:
        slot = all_ref.at[col_at(pos, offset)]
        if key is not None:
            view = slot.at[pl.ds(start, count)]
            pltpu.make_async_remote_copy(
                src_ref=view, dst_ref=view,
                send_sem=send_sems.at[COPY_IDS[key]], recv_sem=recv_sems.at[COPY_IDS[key]],
                device_id=peers[0], device_id_type=MESH,
            ).wait_recv()
        for dim, step, s0, n, target in sends:
            source = (own_ref if key is None else slot).at[pl.ds(s0, n)]
            copy = pltpu.make_async_remote_copy(
                src_ref=source, dst_ref=slot.at[pl.ds(s0, n)],
                send_sem=send_sems.at[COPY_IDS[target]], recv_sem=recv_sems.at[COPY_IDS[target]],
                device_id=neighbour(pos, dim, step), device_id_type=MESH,
            )
            copy.start()
            started.append(copy)
    for copy in started:
        copy.wait_send()
    mine.wait()


def gather_all(own):
    rows, rhs = own.shape
    return pl.pallas_call(
        gather_kernel,
        out_shape=jax.ShapeDtypeStruct((32, rows, rhs), own.dtype),
        in_specs=[pl.BlockSpec(memory_space=pl.ANY)],
        out_specs=pl.BlockSpec(memory_space=pl.ANY),
        scratch_shapes=[
            pltpu.SemaphoreType.DMA((COPIES,)), pltpu.SemaphoreType.DMA((COPIES,)), pltpu.SemaphoreType.DMA,
        ],
        compiler_params=pltpu.CompilerParams(collective_id=0, has_side_effects=True),
        name="gather_all",
    )(own)


def product_kernel(cols_ref, fresh_ref, ptrs_ref, values_ref, all_ref, out_ref, pieces, running, sems):
    slots, size, width = pieces.shape

    def fetch(e):
        return pltpu.make_async_copy(all_ref.at[cols_ref[e]], pieces.at[e], sems.at[e])

    def begin(e, carry):
        fetch(e).start()
        return carry

    lax.fori_loop(0, slots, begin, 0, unroll=8)
    zero = jnp.zeros((size, width), pieces.dtype)

    def group(g, acc):
        first = g * GROUP
        for k in range(GROUP):
            fetch(first + k).wait()
        for k in range(0, GROUP, 2):
            e = first + k
            both = values_ref[:, pl.ds(pl.multiple_of(e * size, 2 * size), 2 * size)]
            right = jnp.concatenate(
                [jnp.concatenate([pieces[e], zero], axis=1), jnp.concatenate([zero, pieces[e + 1]], axis=1)],
                axis=0,
            )
            product = jnp.dot(both, right, preferred_element_type=jnp.float32)
            for j in range(2):
                acc = jnp.where(fresh_ref[e + j] == 1, 0.0, acc) + product[:, j * width:(j + 1) * width]
                running[e + j] = acc
        return acc

    lax.fori_loop(0, slots // GROUP, group, jnp.zeros((size, width), jnp.float32))

    def finish(l, carry):
        end = ptrs_ref[l + 1]
        value = running[jnp.maximum(end - 1, 0)]
        out_ref[l] = jnp.where(end > ptrs_ref[l], value, 0.0)
        return carry

    lax.fori_loop(0, out_ref.shape[0], finish, 0, unroll=8)


def block_products(cols, fresh, ptrs, values, gathered):
    size = values.shape[0]
    slots = cols.shape[0]
    rhs = gathered.shape[-1]
    pieces = gathered.reshape(-1, size, rhs)
    tile_rows = ptrs.shape[0] - 1
    return pl.pallas_call(
        product_kernel,
        out_shape=jax.ShapeDtypeStruct((tile_rows, size, rhs), jnp.float32),
        in_specs=[pl.BlockSpec(memory_space=pltpu.SMEM)] * 3
        + [pl.BlockSpec(memory_space=pltpu.VMEM), pl.BlockSpec(memory_space=pl.ANY)],
        out_specs=pl.BlockSpec(memory_space=pltpu.VMEM),
        scratch_shapes=[
            pltpu.VMEM((slots, size, rhs), jnp.bfloat16),
            pltpu.VMEM((slots, size, rhs), jnp.float32),
            pltpu.SemaphoreType.DMA((slots,)),
        ],
        name="block_products",
    )(cols, fresh, ptrs, values, pieces)


CHUNKS = 8
HALF_CHUNKS = CHUNKS // 2


def reduce_kernel(last, *refs):
    if last:
        part_ref, smoothed_ref, residual_ref, applied_ref, stats_ref = refs[:5]
        scratch = refs[5:]
    else:
        part_ref, smoothed_ref, residual_ref, factor_ref = refs[:4]
        applied_ref, stats_ref, next_ref, half_ref, update_ref = refs[4:9]
        factor, vector, flipped, factor_sems = refs[9:13]
        scratch = refs[13:]
    (from_core, far, relay, landed, mine, others, core_send, core_recv, near_sems,
     relay_send, relay_recv, far_send, far_recv, sum_send, sum_recv) = scratch
    pos = position()
    h, core = pos["h"], pos["core"]
    height = h * 2 + pos["z"]

    def along_z(step, other=0):
        level = (height + step) % 4
        return device_at({**pos, "h": level // 2, "z": level % 2, "core": (core + other) % 2})

    partner = along_z(0, 1)
    groups = [
        [along_z(s, o) for s in range(4) for o in range(2) if s or o],
        [
            device_at({**pos, "x": (pos["x"] + i) % 4, "y": (pos["y"] + j) % 4})
            for i in range(4) for j in range(4) if i or j
        ],
    ]
    barrier = pltpu.get_barrier_semaphore()
    peers = [p for g in groups for p in g]
    for peer in peers:
        pl.semaphore_signal(barrier, inc=1, device_id=peer, device_id_type=MESH)
    if not last:
        factor_loads = factor_copies(factor_ref, factor, factor_sems)
        for copy in reversed(factor_loads):
            copy.start()
    pl.semaphore_wait(barrier, len(peers))

    def send(source, target, send_sem, recv_sem, device):
        copy = pltpu.make_async_remote_copy(
            src_ref=source, dst_ref=target, send_sem=send_sem, recv_sem=recv_sem,
            device_id=device, device_id_type=MESH,
        )
        copy.start()
        return copy

    rows = part_ref.shape[1]
    step_rows = rows // CHUNKS
    spans = [pl.ds(c * step_rows, step_rows) for c in range(CHUNKS)]
    order = [c for both in zip(range(HALF_CHUNKS), range(HALF_CHUNKS, CHUNKS)) for c in both]
    ways = [along_z(1 if c < HALF_CHUNKS else 3) for c in range(CHUNKS)]
    swaps = {
        c: send(part_ref.at[(1 - h) * 2 + 1 - core, spans[c]], from_core.at[0, spans[c]],
                core_send.at[c], core_recv.at[c], partner)
        for c in order
    }
    near = send(part_ref.at[h * 2 + 1 - core], from_core.at[1], near_sems.at[0], near_sems.at[1], partner)
    hops, ends = {}, {}
    ready = []
    for c in order + [None]:
        if c is not None:
            swaps[c].wait_recv()
            total = part_ref[(1 - h) * 2 + core, spans[c], :] + from_core[0, spans[c], :]
            far[c] = total.astype(far.dtype)
            ready.append(c)
        if c is None or len(ready) > 1:
            k = ready.pop(0)
            hops[k] = send(far.at[k], relay.at[k], relay_send.at[k], relay_recv.at[k], ways[k])
    for c in order:
        hops[c].wait_recv()
        ends[c] = send(relay.at[c], landed.at[c], far_send.at[c], far_recv.at[c], ways[c])
    gamma = jnp.sum(residual_ref[...] * smoothed_ref[...], axis=0, keepdims=True)
    near.wait_recv()
    delta = jnp.zeros_like(gamma)
    for c in order:
        span = spans[c]
        local = part_ref[h * 2 + core, span, :] + from_core[1, span, :]
        ends[c].wait_recv()
        value = local + landed[c].astype(jnp.float32)
        applied_ref[span, :] = value
        if not last:
            vector[0, span, :], vector[1, span, :] = split(value)
        delta = delta + jnp.sum(smoothed_ref[span, :] * value, axis=0, keepdims=True)
    total = jnp.concatenate([gamma, delta, jnp.zeros((6, gamma.shape[1]), jnp.float32)], axis=0)
    sums = []
    base = 0
    strips = list(reversed(range(STRIPS)))
    for g, group in enumerate(groups):
        mine[g] = total
        batch = [
            send(mine.at[g], others.at[base + k], sum_send.at[base + k], sum_recv.at[base + k], peer)
            for k, peer in enumerate(group)
        ]
        if not last:
            for i in strips[:1] if g == 0 else strips[1:]:
                factor_loads[i].wait()
                precondition_strip(i, factor, vector, flipped)
        for k, copy in enumerate(batch):
            copy.wait_recv()
            total = total + others[base + k]
        sums += batch
        base += len(group)
    stats_ref[...] = total
    if not last:
        alpha = total[0:1] / total[1:2]
        following = smoothed_ref[...] - alpha * flipped[...].T
        next_ref[...] = following
        half_ref[...] = following.astype(jnp.bfloat16)
        update_ref[...] = residual_ref[...] - alpha * applied_ref[...]
    for copy in list(swaps.values()) + [near] + list(hops.values()) + list(ends.values()) + sums:
        copy.wait_send()


def reduce_all(partial, smoothed, residual, factor=None):
    last = factor is None
    rows, rhs = smoothed.shape
    dma = pltpu.SemaphoreType.DMA
    chunk = pltpu.VMEM((CHUNKS, rows // CHUNKS, rhs), jnp.bfloat16)
    whole = jax.ShapeDtypeStruct((rows, rhs), jnp.float32)
    outs = [whole, jax.ShapeDtypeStruct((8, rhs), jnp.float32)]
    operands = [partial, smoothed, residual]
    specs = [pl.BlockSpec(memory_space=pltpu.VMEM)] * 3
    scratch = []
    if not last:
        outs += [whole, jax.ShapeDtypeStruct((rows, rhs), jnp.bfloat16), whole]
        operands.append(factor)
        specs.append(pl.BlockSpec(memory_space=pl.ANY))
        scratch = [
            pltpu.VMEM((rows, rows), jnp.float32),
            pltpu.VMEM((2, rows, rhs), jnp.bfloat16),
            pltpu.VMEM((rhs, rows), jnp.float32),
            dma((STRIPS,)),
        ]
    scratch += [
        pltpu.VMEM((2, rows, rhs), jnp.float32), chunk, chunk, chunk,
        pltpu.VMEM((2, 8, rhs), jnp.float32), pltpu.VMEM((22, 8, rhs), jnp.float32),
        dma((CHUNKS,)), dma((CHUNKS,)), dma((2,)),
        dma((CHUNKS,)), dma((CHUNKS,)), dma((CHUNKS,)), dma((CHUNKS,)),
        dma((22,)), dma((22,)),
    ]
    return pl.pallas_call(
        functools.partial(reduce_kernel, last),
        out_shape=tuple(outs),
        in_specs=specs,
        out_specs=(pl.BlockSpec(memory_space=pltpu.VMEM),) * len(outs),
        scratch_shapes=scratch,
        compiler_params=pltpu.CompilerParams(collective_id=2 if last else 1, has_side_effects=True),
        name="reduce_last" if last else "reduce_first",
    )(*operands)


def per_device(right_side, block_values, block_cols, row_ptrs, precond):
    slot_count = block_cols.shape[0]
    seg_rows, rhs_count = right_side.shape
    slot_index = jnp.arange(slot_count, dtype=jnp.int32)
    fresh = jnp.any(slot_index[:, None] == row_ptrs[None, :-1], axis=1).astype(jnp.int32)

    def apply(half):
        partial = block_products(block_cols, fresh, row_ptrs, block_values, gather_all(half))
        return partial.reshape(4, seg_rows, rhs_count)

    first, half = precondition(precond, right_side)
    image, stats, second, half, residual = reduce_all(apply(half), first, right_side, precond)
    applied, last_stats = reduce_all(apply(half), second, residual)
    gamma_prev, gamma_now = stats[0], last_stats[0]
    alpha_prev = gamma_prev / stats[1]
    beta = gamma_now / gamma_prev
    alpha = gamma_now / (last_stats[1] - beta * gamma_now / alpha_prev)
    solution = alpha_prev * first + alpha * (second + beta * first)
    residual = residual - alpha * (applied + beta * image)
    return (solution, residual)


def solution(mesh):
    return jax.shard_map(
        per_device,
        mesh=mesh,
        in_specs=(
            P(("row", "col"), None),
            P(None, ("row", "col")),
            P(("row", "col")),
            P(("row", "col")),
            P(("row", "col"), None),
        ),
        out_specs=(P(("row", "col"), None), P(("row", "col"), None)),
        check_vma=False,
    )
```

time: 228 us -> 171 us (0.75)
  matrix products: 27.5 us -> 0 us
  Pallas kernels: 191 us -> 166 us
  other arithmetic: 6.56 us -> 4.22 us
    dot_general x4 -> x0, matrix products: 27.5 us -> none  [the longest x2 15.4 us: per_device(): lax.dot_general(precond, half_step, (((0,), (0,)), ((), ())), precision=l...]
    pallas_call x2, Pallas kernels: 27.2 us -> 13.4 us  [block_products(): pl.pallas_call(product_kernel, out_shape=jax.ShapeDtypeStruct((tile_rows,...]
    pallas_call x2, Pallas kernels: 101 us -> 91.4 us  [gather_all(): pl.pallas_call(gather_kernel, out_shape=jax.ShapeDtypeStruct((32, rows, r...]
    pallas_call x2 -> x3, Pallas kernels: 63.4 us -> 60.8 us  [the longest x2 54.4 us: reduce_all(): pl.pallas_call(functools.partial(reduce_kernel, last), out_shape=tuple(ou...]
where the time goes in v2:
time: 171 us
  Pallas kernels  166 us (97%)
  other arithmetic  4.22 us (2%)
    pallas_call x2, Pallas kernels, gather_all(): pl.pallas_call(gather_kernel, out_shape=jax.ShapeDtypeStruct((32, rows, r...  91.4 us
    pallas_call x2, Pallas kernels, reduce_all(): pl.pallas_call(functools.partial(reduce_kernel, last), out_shape=tuple(ou...  54.4 us
    pallas_call x2, Pallas kernels, block_products(): pl.pallas_call(product_kernel, out_shape=jax.ShapeDtypeStruct((tile_rows,...  13.4 us
    pallas_call x1, Pallas kernels, precondition(): pl.pallas_call(precondition_kernel, out_shape=(jax.ShapeDtypeStruct((rows...  6.42 us

profile of v2, /device:TPU:1, one launch (start us, length us, event | category | flops | bytes accessed | tf_op | source)
XLA Modules:
  0.0 170.6 jit_solution(2776408879174869311)
XLA Ops:
  0.6 0.7 fusion
  1.4 0.5 convert_element_type.3.fresh_ref
  1.9 6.4 %precondition.1 = (f32[1024,128]{1,0:T(8,128)}, bf16[1024,128]{1,0:T(8,128)(2,1)}) custom-call(f32[1024,1024]{1,0:T(8,128)} %refs_3_.1, f32[1024,128]{1,0:T(8,128)} %refs_2_.1), custom_call_target="tpu_custom_call" | custom-call | tf_op jit(solution)/shard_map/precondition/pallas_call | solution.py:163
  8.3 47.5 %gather_all.2 = bf16[32,1024,128]{2,1,0:T(8,128)(2,1)} custom-call(bf16[1024,128]{1,0:T(8,128)(2,1)} %get-tuple-element.11.own_ref), custom_call_target="tpu_custom_call" | custom-call | tf_op jit(solution)/shard_map/gather_all/pallas_call | solution.py:222
  55.9 6.7 %block_products.2 = f32[64,64,128]{2,1,0:T(8,128)} custom-call(s32[112]{0:T(128)} %cols_ref.3, s32[112]{0:T(128)} %convert_element_type.3.fresh_ref, s32[65]{0:T(128)} %ptrs_ref.3, bf16[64,7168]{1,0:T(8,128)(2,1)} %values_ref.3, bf16[512,64,128]{2,1,0:T(8,128)(2,1)} %bitcast.11), custom_call_target="tpu_custom_call" | custom-call | tf_op jit(solution)/shard_map/block_products/pallas_call | solution.py:282
  62.6 28.0 %reduce_first.1 = (f32[1024,128]{1,0:T(8,128)}, f32[8,128]{1,0:T(8,128)}, f32[1024,128]{1,0:T(8,128)}, bf16[1024,128]{1,0:T(8,128)(2,1)}, f32[1024,128]{1,0:T(8,128)}) custom-call(f32[4,1024,128]{2,1,0:T(8,128)} %bitcast.12, f32[1024,128]{1,0:T(8,128)} %get-tuple-element.12.refs_1_, f32[1024,128]{1,0:T(8,128)} %refs_2_.1, f32[1024,1024]{1,0:T(8,128)} %refs_3_.1), custom_call_target="tpu_custom_call" | custom-call | tf_op jit(solution)/shard_map/reduce_first/pallas_call | solution.py:440
  90.6 43.9 %gather_all.3 = bf16[32,1024,128]{2,1,0:T(8,128)(2,1)} custom-call(bf16[1024,128]{1,0:T(8,128)(2,1)} %get-tuple-element.14.own_ref), custom_call_target="tpu_custom_call" | custom-call | tf_op jit(solution)/shard_map/gather_all/pallas_call | solution.py:222
  134.5 0.0 copy-start
  134.5 0.0 copy-start.1
  134.5 0.0 copy-start.2
  134.5 0.0 copy-start.3
  134.5 6.7 %block_products.3 = f32[64,64,128]{2,1,0:T(8,128)} custom-call(s32[112]{0:T(128)} %cols_ref.3, s32[112]{0:T(128)} %convert_element_type.3.fresh_ref, s32[65]{0:T(128)} %ptrs_ref.3, bf16[64,7168]{1,0:T(8,128)(2,1)} %values_ref.3, bf16[512,64,128]{2,1,0:T(8,128)(2,1)} %bitcast.10), custom_call_target="tpu_custom_call" | custom-call | tf_op jit(solution)/shard_map/block_products/pallas_call | solution.py:282
  141.2 26.4 %reduce_last.1 = (f32[1024,128]{1,0:T(8,128)}, f32[8,128]{1,0:T(8,128)}) custom-call(f32[4,1024,128]{2,1,0:T(8,128)} %bitcast.13, f32[1024,128]{1,0:T(8,128)} %get-tuple-element.15.refs_1_, f32[1024,128]{1,0:T(8,128)} %get-tuple-element.16.refs_2_), custom_call_target="tpu_custom_call" | custom-call | tf_op jit(solution)/shard_map/reduce_last/pallas_call | solution.py:440
  167.6 0.8 fusion.1
  168.4 0.0 copy-done
  168.4 0.0 copy-done.1
  168.4 0.0 copy-done.2
  168.4 0.0 copy-done.3
  168.4 2.2 %multiply_subtract_fusion = (f32[1024,128]{1,0:T(8,128)}, f32[1024,128]{1,0:T(8,128)}) fusion(f32[1024,128]{1,0:T(8,128)S(1)} %copy-done.2, f32[1024,128]{1,0:T(8,128)} %get-tuple-element.18, f32[1024,128]{1,0:T(8,128)S(1)} %copy-done.3, f32[128]{0:T(128)S(1)} %bitcast.15, f32[128]{0:T(128)S(1)} %get-tuple-element.20, f32[1024,128]{1,0:T(8,128)S(1)} %copy-done.1, ...), kind=kLoop, calls=%fused_computation | loop fusion | flops 1179648 | bytes 3671552 | tf_op jit(solution)/shard_map/sub | solution.py:469
Async XLA Ops:
  134.5 33.9 %copy-start = (f32[1024,128]{1,0:T(8,128)S(1)}, f32[1024,128]{1,0:T(8,128)}, u32[]{:S(2)}) copy-start(f32[1024,128]{1,0:T(8,128)} %get-tuple-element.12.refs_1_) | copy-start | bytes 1572868
  134.5 33.9 %copy-start.1 = (f32[1024,128]{1,0:T(8,128)S(1)}, f32[1024,128]{1,0:T(8,128)}, u32[]{:S(2)}) copy-start(f32[1024,128]{1,0:T(8,128)} %get-tuple-element.15.refs_1_) | copy-start | bytes 1572868
  134.5 33.9 %copy-start.2 = (f32[1024,128]{1,0:T(8,128)S(1)}, f32[1024,128]{1,0:T(8,128)}, u32[]{:S(2)}) copy-start(f32[1024,128]{1,0:T(8,128)} %get-tuple-element.16.refs_2_) | copy-start | bytes 1572868
  134.5 33.9 %copy-start.3 = (f32[1024,128]{1,0:T(8,128)S(1)}, f32[1024,128]{1,0:T(8,128)}, u32[]{:S(2)}) copy-start(f32[1024,128]{1,0:T(8,128)} %get-tuple-element.19) | copy-start | bytes 1572868
